TPU v7x, 32 devices: a whole 2x2x4 slice. The times are simulated.
32 devices in a mesh: grp: 2 (over core), rep: 16 (over z, y, x).
Axes of the slice: x: 2, y: 2, z: 4, core: 2. Of those that a mesh axis runs over, the one named last changes fastest.
Arguments:
- tokens: bfloat16 [16, 1024, 1152], P('rep', 'grp'), may hold values from -6 to 6
- cotangent: bfloat16 [16, 1024, 1152], P('rep', 'grp'), may hold values from -6 to 6
- segment_ids: int32 [16, 1024], P('rep'), may hold values from 0 to 3, never falling along the last dimension, each value on 1 to 800 neighbouring positions
- adapter_ids: int32 [16], P('rep'), may hold values from 0 to 7
- norm_gains: bfloat16 [2, 1152], P(None, 'grp'), may hold values from 0.5 to 1.5
- frozen_qkv: bfloat16 [1152, 1920], P('grp'), may hold values from -0.1875 to 0.1875
- frozen_out: bfloat16 [1152, 1152], P('grp'), may hold values from -1.5 to 1.5
- frozen_gate_up: bfloat16 [1152, 6144], P('grp'), may hold values from -0.1875 to 0.1875
- frozen_down: bfloat16 [3072, 1152], P('grp'), may hold values from -0.109375 to 0.109375
- lower_mats: bfloat16 [6, 8, 1152, 16], replicated, may hold values from -0.1875 to 0.1875
- lower_down: bfloat16 [8, 3072, 16], replicated, may hold values from -0.109375 to 0.109375
- upper_width: bfloat16 [3, 8, 16, 1152], replicated, may hold values from -1 to 1
- upper_keys: bfloat16 [2, 8, 16, 384], replicated, may hold values from -1 to 1
- upper_hidden: bfloat16 [2, 8, 16, 3072], replicated, may hold values from -1 to 1
Outputs:
- layer_out: bfloat16 [16, 1024, 1152], P('rep', 'grp')
- input_grad: bfloat16 [16, 1024, 1152], P('rep', 'grp')
- lower_grad: float32 [6, 8, 1152, 16], P(None, 'grp', 'rep')
- lower_down_grad: float32 [8, 3072, 16], P('grp', 'rep')
- upper_width_grad: float32 [3, 8, 16, 1152], P(None, 'grp', None, 'rep')
- upper_keys_grad: float32 [2, 8, 16, 384], P(None, 'grp', None, 'rep')
- upper_hidden_grad: float32 [2, 8, 16, 3072], P(None, 'grp', None, 'rep')
Inputs may be any that keep to these rules, and one draw needn't show every extreme that they name: `segment_ids`: within each sequence the ids never fall, each document has 1 to 800 positions, and one has exactly 800.
All inputs are finite; a program needn't handle non-finite values.
Results may differ from a plain program's by a relative error of at most 0.018.
Values may be sent and summed in bfloat16 or wider, within the bound.
No kernel may reach another device: no remote copies, remote signals or barrier semaphores. Data moves between devices by JAX's collectives and lax.ppermute only.
A program may use at most 192 MiB of HBM per device.

v0:
```python
import jax
import jax.numpy as jnp
from jax import lax
from jax.sharding import PartitionSpec as P

D = 1152
H = 18
KVH = 6
HD = 64
FF = 3072
R = 16
NAD = 8
KV = 384


epsilon = 1e-05
theta_base = 10000.0
masked_value = -1e30


def passed_along(value, axis, by):
    size = lax.axis_size(axis)
    pairs = [(i, i + by) for i in range(size) if 0 <= i + by < size]
    return lax.ppermute(value, axis, pairs)


def contract(form, left, right):
    return jnp.einsum(form, left, right, preferred_element_type=jnp.float32)


def normalize(rows, gain_row):
    return rows * lax.rsqrt(jnp.mean(rows * rows, axis=-1, keepdims=True) + epsilon) * gain_row


def positions_of(segments):
    places = jnp.arange(segments.shape[0], dtype=jnp.int32)
    change = jnp.concatenate([jnp.ones((1,), jnp.bool_), segments[1:] != segments[:-1]])
    starts = lax.cummax(jnp.where(change, places, 0), axis=0)
    return places - starts


def angles(positions, head_size):
    half_size = head_size // 2
    freqs = theta_base ** (-jnp.arange(half_size, dtype=jnp.float32) * 2.0 / head_size)
    turned = positions.astype(jnp.float32)[:, None] * freqs[None, :]
    return (jnp.cos(turned)[:, None, :], jnp.sin(turned)[:, None, :])


def rotate(rows, cosine, sine):
    half_size = rows.shape[-1] // 2
    first = rows[..., :half_size]
    second = rows[..., half_size:]
    return jnp.concatenate(
        [first * cosine - second * sine, second * cosine + first * sine], axis=-1
    )


def spread_out(local_grad, picked, lead):
    if lead:
        return picked[None, :, None, None] * local_grad[:, None]
    return picked[:, None, None] * local_grad[None]


def per_device(
    tokens,
    cotangent,
    segment_ids,
    adapter_ids,
    norm_gains,
    frozen_qkv,
    frozen_out,
    frozen_gate_up,
    frozen_down,
    lower_mats,
    lower_down,
    upper_width,
    upper_keys,
    upper_hidden,
):
    chosen = adapter_ids[0]
    segments = segment_ids[0]
    tok_rows = tokens.shape[1]
    groups = H // KVH
    factor = HD ** (-0.5)
    offset = lax.axis_index("grp") * tok_rows
    gains_all, qkv_full, out_full, gate_up_full, down_full = (
        lax.all_gather(norm_gains, "grp", axis=1, tiled=True),
        lax.all_gather(frozen_qkv, "grp", axis=0, tiled=True),
        lax.all_gather(frozen_out, "grp", axis=0, tiled=True),
        lax.all_gather(frozen_gate_up, "grp", axis=0, tiled=True),
        lax.all_gather(frozen_down, "grp", axis=0, tiled=True),
    )
    lower_pick = lax.dynamic_index_in_dim(lower_mats, chosen, 1, keepdims=False)
    lower_last = lax.dynamic_index_in_dim(lower_down, chosen, 0, keepdims=False)
    width_pick = lax.dynamic_index_in_dim(upper_width, chosen, 1, keepdims=False)
    keys_pick = lax.dynamic_index_in_dim(upper_keys, chosen, 1, keepdims=False)
    hidden_pick = lax.dynamic_index_in_dim(upper_hidden, chosen, 1, keepdims=False)
    picked = (jnp.arange(NAD, dtype=jnp.int32) == chosen).astype(jnp.float32)
    positions = lax.dynamic_slice_in_dim(positions_of(segments), offset, tok_rows)
    cosine, sine = angles(positions, HD)
    padded_segs = jnp.concatenate([jnp.full((tok_rows,), -1, jnp.int32), segments])
    key_segs = lax.dynamic_slice_in_dim(padded_segs, offset, 2 * tok_rows)
    query_segs = lax.dynamic_slice_in_dim(segments, offset, tok_rows)
    query_place = offset + jnp.arange(tok_rows, dtype=jnp.int32)
    key_place = offset - tok_rows + jnp.arange(2 * tok_rows, dtype=jnp.int32)
    allowed = (key_place[None, :] <= query_place[:, None]) & (
        key_segs[None, :] == query_segs[:, None]
    )
    hidden = tokens[0].astype(jnp.float32)
    gain_one = gains_all[0].astype(jnp.float32)
    gain_two = gains_all[1].astype(jnp.float32)
    normed = normalize(hidden, gain_one).astype(jnp.bfloat16)
    qkv_lower = jnp.concatenate([lower_pick[0], lower_pick[1], lower_pick[2]], axis=1)
    inner_qkv = jnp.dot(normed, qkv_lower, preferred_element_type=jnp.float32).astype(jnp.bfloat16)
    base_qkv = jnp.dot(normed, qkv_full, preferred_element_type=jnp.float32)
    query_lin = base_qkv[:, :D] + jnp.dot(
        inner_qkv[:, :R], width_pick[0], preferred_element_type=jnp.float32
    )
    key_lin = base_qkv[:, D : D + KV] + jnp.dot(
        inner_qkv[:, R : 2 * R], keys_pick[0], preferred_element_type=jnp.float32
    )
    value_lin = base_qkv[:, D + KV :] + jnp.dot(
        inner_qkv[:, 2 * R :], keys_pick[1], preferred_element_type=jnp.float32
    )
    queries = rotate(query_lin.reshape(tok_rows, H, HD), cosine, sine).astype(jnp.bfloat16)
    key_flat = (
        rotate(key_lin.reshape(tok_rows, KVH, HD), cosine, sine)
        .astype(jnp.bfloat16)
        .reshape(tok_rows, KV)
    )
    value_flat = value_lin.astype(jnp.bfloat16)
    prev_keys, prev_values = passed_along((key_flat, value_flat), "grp", 1)
    all_keys = (
        jnp.concatenate([prev_keys, key_flat], axis=0)
        .reshape(2 * tok_rows, KVH, HD)
        .transpose(1, 0, 2)
    )
    all_values = (
        jnp.concatenate([prev_values, value_flat], axis=0)
        .reshape(2 * tok_rows, KVH, HD)
        .transpose(1, 0, 2)
    )
    grouped = queries.reshape(tok_rows, KVH, groups, HD).transpose(1, 0, 2, 3)

    def head_forward(operands):
        query_block, key_block, value_block = operands
        scores = contract("tgd,sd->gts", query_block, key_block) * factor
        scores = jnp.where(allowed[None], scores, masked_value)
        row_max = jnp.max(scores, axis=-1, keepdims=True)
        weights = jnp.exp(scores - row_max)
        row_total = jnp.sum(weights, axis=-1, keepdims=True)
        chances = (weights / row_total).astype(jnp.bfloat16)
        blended = contract("gts,sd->tgd", chances, value_block)
        return (blended, row_max[..., 0] + jnp.log(row_total[..., 0]))

    blended, log_total = lax.map(head_forward, (grouped, all_keys, all_values))
    attn_mix = blended.transpose(1, 0, 2, 3).reshape(tok_rows, D).astype(jnp.bfloat16)
    inner_out = jnp.dot(attn_mix, lower_pick[3], preferred_element_type=jnp.float32).astype(
        jnp.bfloat16
    )
    branch = jnp.dot(attn_mix, out_full, preferred_element_type=jnp.float32) + jnp.dot(
        inner_out, width_pick[1], preferred_element_type=jnp.float32
    )
    middle = hidden + branch
    normed_two = normalize(middle, gain_two).astype(jnp.bfloat16)
    ff_lower = jnp.concatenate([lower_pick[4], lower_pick[5]], axis=1)
    inner_ff = jnp.dot(normed_two, ff_lower, preferred_element_type=jnp.float32).astype(
        jnp.bfloat16
    )
    base_ff = jnp.dot(normed_two, gate_up_full, preferred_element_type=jnp.float32)
    gate_lin = base_ff[:, :FF] + jnp.dot(
        inner_ff[:, :R], hidden_pick[0], preferred_element_type=jnp.float32
    )
    up_lin = base_ff[:, FF:] + jnp.dot(
        inner_ff[:, R:], hidden_pick[1], preferred_element_type=jnp.float32
    )
    active = (jax.nn.silu(gate_lin) * up_lin).astype(jnp.bfloat16)
    inner_down = jnp.dot(active, lower_last, preferred_element_type=jnp.float32).astype(
        jnp.bfloat16
    )
    result = (
        middle
        + jnp.dot(active, down_full, preferred_element_type=jnp.float32)
        + jnp.dot(inner_down, width_pick[2], preferred_element_type=jnp.float32)
    )
    layer_out = result.astype(jnp.bfloat16)[None]
    gains_all, qkv_full, out_full, gate_up_full, down_full = (
        lax.all_gather(norm_gains, "grp", axis=1, tiled=True),
        lax.all_gather(frozen_qkv, "grp", axis=0, tiled=True),
        lax.all_gather(frozen_out, "grp", axis=0, tiled=True),
        lax.all_gather(frozen_gate_up, "grp", axis=0, tiled=True),
        lax.all_gather(frozen_down, "grp", axis=0, tiled=True),
    )
    gain_one = gains_all[0].astype(jnp.float32)
    gain_two = gains_all[1].astype(jnp.float32)
    cot_rows = cotangent[0]
    grad_out = cot_rows.astype(jnp.float32)
    width_down_grad = contract("tr,td->rd", inner_down, cot_rows)
    grad_inner_down = contract("td,rd->tr", cot_rows, width_pick[2]).astype(jnp.bfloat16)
    down_lower_grad = contract("tf,tr->fr", active, grad_inner_down)
    grad_active = contract("td,fd->tf", cot_rows, down_full) + contract(
        "tr,fr->tf", grad_inner_down, lower_last
    )
    sigmoid_gate = jax.nn.sigmoid(gate_lin)
    grad_gate = (
        grad_active * up_lin * sigmoid_gate * (1.0 + gate_lin * (1.0 - sigmoid_gate))
    ).astype(jnp.bfloat16)
    grad_up = (grad_active * gate_lin * sigmoid_gate).astype(jnp.bfloat16)
    hidden_local = jnp.stack(
        [
            contract("tr,tf->rf", inner_ff[:, :R], grad_gate),
            contract("tr,tf->rf", inner_ff[:, R:], grad_up),
        ]
    )
    grad_inner_ff = jnp.concatenate(
        [
            contract("tf,rf->tr", grad_gate, hidden_pick[0]),
            contract("tf,rf->tr", grad_up, hidden_pick[1]),
        ],
        axis=1,
    ).astype(jnp.bfloat16)
    ff_lower_grad = contract("td,tr->dr", normed_two, grad_inner_ff)
    grad_ff = jnp.concatenate([grad_gate, grad_up], axis=1)
    grad_normed_two = contract("tf,df->td", grad_ff, gate_up_full) + contract(
        "tr,dr->td", grad_inner_ff, ff_lower
    )
    norm_two_back = jax.vjp(lambda rows: normalize(rows, gain_two), middle)[1]
    grad_middle = grad_out + norm_two_back(grad_normed_two)[0]
    ffn_lower_local = ff_lower_grad.reshape(D, 2, R).transpose(1, 0, 2)
    grad_branch = grad_middle.astype(jnp.bfloat16)
    width_out_grad = contract("tr,td->rd", inner_out, grad_branch)
    grad_inner_out = contract("td,rd->tr", grad_branch, width_pick[1]).astype(jnp.bfloat16)
    out_lower_grad = contract("td,tr->dr", attn_mix, grad_inner_out)
    grad_mix = (
        contract("te,de->td", grad_branch, out_full)
        + contract("tr,dr->td", grad_inner_out, lower_pick[3])
    ).astype(jnp.bfloat16)
    grad_grouped = grad_mix.reshape(tok_rows, KVH, groups, HD).transpose(1, 0, 2, 3)

    def head_backward(operands):
        query_block, key_block, value_block, grad_block, log_block = operands
        scores = contract("tgd,sd->gts", query_block, key_block) * factor
        chances = jnp.where(allowed[None], jnp.exp(scores - log_block[..., None]), 0.0)
        grad_chances = contract("tgd,sd->gts", grad_block, value_block)
        grad_scores = (
            chances * (grad_chances - jnp.sum(chances * grad_chances, axis=-1, keepdims=True))
        ).astype(jnp.bfloat16)
        grad_query = contract("gts,sd->tgd", grad_scores, key_block) * factor
        grad_key = contract("gts,tgd->sd", grad_scores, query_block) * factor
        grad_value = contract("gts,tgd->sd", chances.astype(jnp.bfloat16), grad_block)
        return (grad_query, grad_key, grad_value)

    grad_queries, grad_keys, grad_values = lax.map(
        head_backward, (grouped, all_keys, all_values, grad_grouped, log_total)
    )
    grad_queries = grad_queries.transpose(1, 0, 2, 3).reshape(tok_rows, H, HD)
    grad_keys = grad_keys.transpose(1, 0, 2).reshape(2 * tok_rows, KV)
    grad_values = grad_values.transpose(1, 0, 2).reshape(2 * tok_rows, KV)
    back_keys, back_values = (
        passed_along(grad_keys[:tok_rows].astype(jnp.bfloat16), "grp", -1).astype(jnp.float32),
        passed_along(grad_values[:tok_rows].astype(jnp.bfloat16), "grp", -1).astype(jnp.float32),
    )
    grad_key_sum = grad_keys[tok_rows:] + back_keys
    grad_value_sum = grad_values[tok_rows:] + back_values
    grad_query_lin = rotate(grad_queries, cosine, -sine).reshape(tok_rows, D).astype(jnp.bfloat16)
    grad_key_lin = (
        rotate(grad_key_sum.reshape(tok_rows, KVH, HD), cosine, -sine)
        .reshape(tok_rows, KV)
        .astype(jnp.bfloat16)
    )
    grad_value_lin = grad_value_sum.astype(jnp.bfloat16)
    width_query_grad = contract("tr,td->rd", inner_qkv[:, :R], grad_query_lin)
    keys_local = jnp.stack(
        [
            contract("tr,td->rd", inner_qkv[:, R : 2 * R], grad_key_lin),
            contract("tr,td->rd", inner_qkv[:, 2 * R :], grad_value_lin),
        ]
    )
    grad_inner_qkv = jnp.concatenate(
        [
            contract("td,rd->tr", grad_query_lin, width_pick[0]),
            contract("td,rd->tr", grad_key_lin, keys_pick[0]),
            contract("td,rd->tr", grad_value_lin, keys_pick[1]),
        ],
        axis=1,
    ).astype(jnp.bfloat16)
    qkv_lower_grad = contract("td,tr->dr", normed, grad_inner_qkv)
    grad_qkv = jnp.concatenate([grad_query_lin, grad_key_lin, grad_value_lin], axis=1)
    grad_normed = contract("te,de->td", grad_qkv, qkv_full) + contract(
        "tr,dr->td", grad_inner_qkv, qkv_lower
    )
    norm_one_back = jax.vjp(lambda rows: normalize(rows, gain_one), hidden)[1]
    grad_hidden = grad_middle + norm_one_back(grad_normed)[0]
    input_grad = grad_hidden.astype(jnp.bfloat16)[None]
    attn_lower_local = jnp.concatenate(
        [qkv_lower_grad.reshape(D, 3, R).transpose(1, 0, 2), out_lower_grad[None]], axis=0
    )
    attn_width_local = jnp.stack([width_query_grad, width_out_grad])
    lower_local = jnp.concatenate([attn_lower_local, ffn_lower_local], axis=0)
    width_local = jnp.concatenate([attn_width_local, width_down_grad[None]], axis=0)
    lower_dense = spread_out(lower_local, picked, True)
    down_dense = spread_out(down_lower_grad, picked, False)
    width_dense = spread_out(width_local, picked, True)
    keys_dense = spread_out(keys_local, picked, True)
    hidden_dense = spread_out(hidden_local, picked, True)
    lower_part, down_part, width_part, keys_part, hidden_part = (
        lax.psum_scatter(
            lower_dense.astype(jnp.bfloat16), "grp", scatter_dimension=1, tiled=True
        ).astype(jnp.float32),
        lax.psum_scatter(
            down_dense.astype(jnp.bfloat16), "grp", scatter_dimension=0, tiled=True
        ).astype(jnp.float32),
        lax.psum_scatter(
            width_dense.astype(jnp.bfloat16), "grp", scatter_dimension=1, tiled=True
        ).astype(jnp.float32),
        lax.psum_scatter(
            keys_dense.astype(jnp.bfloat16), "grp", scatter_dimension=1, tiled=True
        ).astype(jnp.float32),
        lax.psum_scatter(
            hidden_dense.astype(jnp.bfloat16), "grp", scatter_dimension=1, tiled=True
        ).astype(jnp.float32),
    )
    lower_sum, down_sum, width_sum, keys_sum, hidden_sum = (
        lax.psum_scatter(lower_part, "rep", scatter_dimension=2, tiled=True),
        lax.psum_scatter(down_part, "rep", scatter_dimension=1, tiled=True),
        lax.psum_scatter(width_part, "rep", scatter_dimension=3, tiled=True),
        lax.psum_scatter(keys_part, "rep", scatter_dimension=3, tiled=True),
        lax.psum_scatter(hidden_part, "rep", scatter_dimension=3, tiled=True),
    )
    return (layer_out, input_grad, lower_sum, down_sum, width_sum, keys_sum, hidden_sum)


def solution(mesh):
    return jax.shard_map(
        per_device,
        mesh=mesh,
        in_specs=(
            P("rep", "grp", None),
            P("rep", "grp", None),
            P("rep", None),
            P("rep"),
            P(None, "grp"),
            P("grp", None),
            P("grp", None),
            P("grp", None),
            P("grp", None),
            P(),
            P(),
            P(),
            P(),
            P(),
        ),
        out_specs=(
            P("rep", "grp", None),
            P("rep", "grp", None),
            P(None, "grp", "rep", None),
            P("grp", "rep", None),
            P(None, "grp", None, "rep"),
            P(None, "grp", None, "rep"),
            P(None, "grp", None, "rep"),
        ),
        check_vma=False,
    )
```

profile of v0, /device:TPU:0, one launch (start us, length us, event | category | flops | bytes accessed | tf_op | source)
XLA Modules:
  0.0 872.5 jit_solution(11783414570455950583)
XLA Ops:
  26.3 5.2 fusion.113
  37.0 3.4 copy.57
  53.0 48.3 %while.30 = (s32[]{:T(128)}, bf16[6,512,3,64]{1,3,2,0:T(8,128)(2,1)S(1)}, f32[6,3,512]{2,1,0:T(4,128)}, bf16[6,1024,64]{1,2,0:T(8,128)(2,1)}, bf16[6,1024,64]{1,...) while((s32[]{:T(128)}, ...), condition=%wide.region_6.7_spmd.clone.clone, body=%wide.region_3.6_spmd.clone.sunk.clone | while | flops 423098880 | bytes 21893732 | solution.py:156
  58.2 2.9 fusion.245
  66.2 2.9 fusion.245
  74.2 3.0 fusion.245
  82.4 2.9 fusion.245
  90.4 2.9 fusion.245
  98.4 2.9 fusion.245
  103.1 3.7 fusion.165
  112.2 6.5 fusion.104
  118.7 4.5 convolution_add_fusion
  123.2 14.7 %fusion.166 = f32[512,6144]{1,0:T(8,128)} fusion(bf16[512,1152]{1,0:T(8,128)(2,1)} %copy-done.13, bf16[1152,6144]{1,0:T(8,128)(2,1)} %all-gather.10.cloned.1.call-done), kind=kOutput, calls=%fused_computation.274 | convolution fusion | flops 7247757312 | bytes 27918336 | tf_op jit(solution)/shard_map/dot_general | solution.py:170
  137.9 3.9 slice_add_fusion
  142.5 6.9 multiply_convert_fusion.1
  156.6 16.8 %multiply_reduce_fusion = (f32[512]{0:T(512)S(1)}, f32[512,1152]{1,0:T(8,128)}) fusion(f32[512,1152]{1,0:T(8,128)} %copy-done.4, f32[1152]{0:T(1024)S(1)} %copy-done.63, f32[512,1152]{1,0:T(8,128)} %fusion.119, bf16[1152,6144]{1,0:T(8,128)(2,1)} %all-gather.10.cloned.1.call-done, bf16[512,3072]{1,0:T(8,128)(2,1)} %copy-done.7, bf16[512,3072]{1,0:T(8,128)(2,1)} %copy-done.6), kind=kOutput, calls=%fused_computation.114 | convolution fusion | flops 7262699008 | bytes 27531776 | tf_op jit(solution)/shard_map/tf,df->td/dot_general | solution.py:28
  173.4 2.9 fusion.88
  183.6 94.3 %while.31 = (s32[]{:T(128)}, f32[6,512,3,64]{1,3,2,0:T(8,128)}, f32[6,1024,64]{1,2,0:T(8,128)}, f32[6,1024,64]{1,2,0:T(8,128)}, bf16[6,1024,64]{1,2,0:T(8,128)(2...) while((s32[]{:T(128)}, f32[6,512,3,64]{1,3,2,0:T(8,128)}, ...), condition=%wide.region_11.12_spmd.clone.clone, body=%wide.region_9.11_spmd.clone.sunk.clone | while | flops 1031961088 | bytes 51440768 | solution.py:253
  187.3 3.0 fusion.255
  196.3 3.1 fusion.259
  202.9 3.0 fusion.255
  212.0 3.1 fusion.259
  218.6 3.0 fusion.255
  225.0 2.7 fusion.258
  227.7 3.2 fusion.259
  234.3 3.0 fusion.255
  240.6 2.7 fusion.258
  243.4 3.2 fusion.259
  250.0 3.0 fusion.255
  256.3 2.7 fusion.258
  259.0 3.1 fusion.259
  265.6 3.0 fusion.255
  272.0 2.7 fusion.258
  274.7 3.1 fusion.259
  307.4 3.1 reduce-scatter.25.cloned.1.call-done
  310.6 4.8 copy.68
  315.3 5.8 reshape.316
  322.5 21.8 %all-reduce.14.cloned.1.call-done = (bf16[6,8,1152,16]{2,3,1,0:T(8,128)(2,1)}, bf16[2,8,16,384]{3,2,1,0:T(8,128)(2,1)}, bf16[3,8,16,1152]{3,2,1,0:T(8,128)(2,1)}, bf16[2,8,16,3072]{3,2,1,0:T(8,128)(2,1)}) async-done(((bf16[6,8,1152,16]{2,3,1,0:T(8,128)(2,1)}, bf16[2,8,16,384]{3,2,1,0:T(8,128)(2,1)}, bf16[3,8,16,1152]{3,2,1,0:T(8,128)(2,1)}, bf16[2,8,16,3072]{3,2,1,0:T(8,128)(2,1)}), ...) | async-done | bytes 4423696
  345.3 5.2 copy.72
  350.5 6.5 reshape.320
  363.7 8.6 copy.80
  372.3 11.4 %reshape.328 = f32[3072,128]{1,0:T(8,128)} reshape(f32[3072,2,4,16]{3,2,1,0:T(4,128)} %bitcast.448) | data formatting | bytes 3145728
  383.8 8.9 %convolution_add_fusion.6 = f32[512,1152]{1,0:T(8,128)S(1)} fusion(f32[512,1152]{1,0:T(8,128)} %copy-done.4, bf16[512,3072]{1,0:T(8,128)(2,1)} %get-tuple-element.221, bf16[3072,1152]{1,0:T(8,128)(2,1)} %all-gather.12.cloned.1.call-done), kind=kOutput, calls=%fused_computation.93 | convolution fusion | flops 3624468480 | bytes 14942208 | tf_op jit(solution)/shard_map/dot_general | solution.py:183
  395.1 5.2 fusion.91
  403.7 71.9 %reduce-scatter.27.cloned.1.call-done = f32[192,64]{1,0:T(8,128)} async-done(((f32[3072,64]{1,0:T(8,128)}), f32[192,64]{1,0:T(8,128)}) %reduce-scatter.27.cloned.1.call-update) | async-done | bytes 49168
  477.5 126.9 %reduce-scatter.29.cloned.1.call-done = f32[72,192]{1,0:T(8,128)} async-done(((f32[1152,192]{1,0:T(8,128)}), f32[72,192]{1,0:T(8,128)}) %reduce-scatter.29.cloned.1.call-update) | async-done | bytes 55312
  606.4 128.1 %all-reduce.12.cloned.1.call-done = (f32[6,4,1152,16]{2,3,1,0:T(8,128)}, f32[2,4,16,384]{3,2,1,0:T(8,128)}) async-done(((f32[6,4,1152,16]{2,3,1,0:T(8,128)}, f32[2,4,16,384]{3,2,1,0:T(8,128)}), (f32[6,4,1152,16]{2,3,1,0:T(8,128)}, f32[2,4,16,384]{3,2,1,0:T(8,128)})) %all-reduce.12.cloned.1.call-update) | async-done | bytes 1966096
  737.9 125.0 %reduce-scatter.31.cloned.1.call-done = f32[192,128]{1,0:T(8,128)} async-done(((f32[3072,128]{1,0:T(8,128)}), f32[192,128]{1,0:T(8,128)}) %reduce-scatter.31.cloned.1.call-update) | async-done | bytes 98320
  (349 shorter events, 186.9 us)
Async XLA Ops:
  7.2 130.8 %copy-start = (bf16[2,8,16,3072]{3,2,1,0:T(8,128)(2,1)S(1)}, bf16[2,8,16,3072]{3,2,1,0:T(8,128)(2,1)}, u32[]{:S(2)}) copy-start(bf16[2,8,16,3072]{3,2,1,0:T(8,128)(2,1)} %param.31) | copy-start | bytes 4718596
  7.2 19.1 %all-gather.6.cloned.1.call-start = ((), (), s32[]{:S(2)}) async-start(), calls=%async_computation.4 | async-start | bytes 6635520 | tf_op jit(solution)/shard_map/all_gather | solution.py:88
  7.9 95.2 %all-gather.8.cloned.1.call-start = ((), (), s32[]{:S(2)}) async-start(), calls=%async_computation.5 | async-start | bytes 3981312 | tf_op jit(solution)/shard_map/all_gather | solution.py:89
  8.7 103.5 %all-gather.12.cloned.1.call-start = ((), (), s32[]{:S(2)}) async-start(), calls=%async_computation.7 | async-start | bytes 10616832 | tf_op jit(solution)/shard_map/all_gather | solution.py:91
  9.4 113.8 %all-gather.10.cloned.1.call-start = ((), (), s32[]{:S(2)}) async-start(), calls=%async_computation.6 | async-start | bytes 21233664 | tf_op jit(solution)/shard_map/all_gather | solution.py:90
  10.0 5.2 copy-start.57
  10.0 300.6 %reduce-scatter.25.cloned.1.call-start = ((), (), s32[]{:S(2)}) async-start(), calls=%async_computation.8 | async-start | bytes 1179648 | tf_op jit(solution)/shard_map/reduce_scatter | solution.py:310
  13.6 12.8 %copy-start.59 = (f32[1152]{0:T(1024)}, f32[1152]{0:T(1024)S(1)}, u32[]{:S(2)}) copy-start(f32[1152]{0:T(1024)S(1)} %get-tuple-element.163) | copy-start | bytes 13828
  15.2 16.3 %copy-start.72 = (f32[512]{0:T(512)}, f32[512]{0:T(512)S(1)}, u32[]{:S(2)}) copy-start(f32[512]{0:T(512)S(1)} %fusion.152) | copy-start | bytes 6148
  22.0 9.5 %copy-start.47 = (bf16[1152,16]{0,1:T(8,128)(2,1)}, bf16[1152,16]{0,1:T(8,128)(2,1)S(1)}, u32[]{:S(2)}) copy-start(bf16[1152,16]{0,1:T(8,128)(2,1)S(1)} %get-tuple-element.228) | copy-start | bytes 110596
  22.0 9.5 %copy-start.49 = (bf16[1152,16]{0,1:T(8,128)(2,1)}, bf16[1152,16]{0,1:T(8,128)(2,1)S(1)}, u32[]{:S(2)}) copy-start(bf16[1152,16]{0,1:T(8,128)(2,1)S(1)} %get-tuple-element.229) | copy-start | bytes 110596
  22.0 9.5 %copy-start.51 = (bf16[1152,16]{0,1:T(8,128)(2,1)}, bf16[1152,16]{0,1:T(8,128)(2,1)S(1)}, u32[]{:S(2)}) copy-start(bf16[1152,16]{0,1:T(8,128)(2,1)S(1)} %get-tuple-element.230) | copy-start | bytes 110596
  24.0 7.6 copy-start.39
  42.8 6.7 collective-permute-start.1
  44.9 4.7 collective-permute-start
  101.4 5.4 copy-start.8
  112.2 6.5 copy-start.41
  123.2 14.7 %copy-start.34 = (bf16[512,32]{0,1:T(8,128)(2,1)S(1)}, bf16[512,32]{0,1:T(8,128)(2,1)}, u32[]{:S(2)}) copy-start(bf16[512,32]{0,1:T(8,128)(2,1)} %convolution_convert_fusion.1) | copy-start | bytes 98308
  137.9 4.6 copy-start.17
  156.6 16.8 %copy-start.69 = (f32[512]{0:T(512)S(1)}, f32[512]{0:T(512)}, u32[]{:S(2)}) copy-start(f32[512]{0:T(512)} %copy-done.68) | copy-start | bytes 6148
  156.6 16.8 %copy-start.65 = (f32[512]{0:T(512)S(1)}, f32[512]{0:T(512)}, u32[]{:S(2)}) copy-start(f32[512]{0:T(512)} %copy-done.64) | copy-start | bytes 6148
  173.4 4.3 copy-start.44
  277.9 7.3 copy-start.20
  277.9 7.3 copy-start.21
  277.9 7.3 copy-start.26
  285.7 5.7 copy-start.15
  285.7 4.6 copy-start.9
  285.7 5.7 copy-start.5
  294.1 6.4 collective-permute-start.2
  295.4 6.7 collective-permute-start.3
  299.3 44.9 %all-reduce.14.cloned.1.call-start = ((), (), s32[]{:S(2)}) async-start(), calls=%async_computation.13 | async-start | bytes 8847360
  300.8 4.3 copy-start.11
  300.8 4.3 copy-start.60
  300.8 4.3 copy-start.73
  307.4 168.2 %reduce-scatter.27.cloned.1.call-start = ((), (), s32[]{:S(2)}) async-start(), calls=%async_computation.9 | async-start | bytes 1671168
  315.3 5.9 copy-start.77
  321.2 283.2 %reduce-scatter.29.cloned.1.call-start = ((), (), s32[]{:S(2)}) async-start(), calls=%async_computation.10 | async-start | bytes 1253376
  350.5 6.6 copy-start.58
  357.0 377.5 %all-reduce.12.cloned.1.call-start = ((), (), s32[]{:S(2)}) async-start(), calls=%async_computation.12 | async-start | bytes 3932160
  360.4 502.5 %reduce-scatter.31.cloned.1.call-start = ((), (), s32[]{:S(2)}) async-start(), calls=%async_computation.11 | async-start | bytes 1671168
  395.0 5.3 copy-start.46
  395.0 5.3 copy-start.48
  395.0 5.3 copy-start.50
  395.0 5.3 copy-start.52
  395.0 5.3 copy-start.54
  395.1 5.3 copy-start.56
  395.1 5.3 copy-start.61
  402.1 463.3 %copy-start.1 = (bf16[2,8,16,3072]{3,2,1,0:T(8,128)(2,1)S(1)}, bf16[2,8,16,3072]{3,2,1,0:T(8,128)(2,1)}, u32[]{:S(2)}) copy-start(bf16[2,8,16,3072]{3,2,1,0:T(8,128)(2,1)} %param.31) | copy-start | bytes 4718596
  (44 other events, 103.6 us)
Sparse Core Ops, SparseCore 0:
  9.6 16.6 all-gather.5
  27.8 12.5 all-gather.7
  42.0 19.1 all-gather.11
  62.6 27.5 all-gather.9
  299.4 11.0 reduce-scatter.24
  314.1 30.1 all-reduce.13
  349.8 125.7 reduce-scatter.26
  481.0 123.3 reduce-scatter.28
  611.4 123.0 all-reduce.11
  739.1 123.7 reduce-scatter.30
where the time goes:
time: 880 us; the launch traced here: 872 us
  waiting for transfers between devices  482 us (55%)
  matrix products  220 us (25%)
  local copies, waits for them, and re-layouts  81.2 us (9%)
  other arithmetic  62.2 us (7%)
  between operations  18.1 us (2%)
    unnamed x15, waiting for transfers between devices  476 us
    dot_general x68, matrix products, contract(): return jnp.einsum(form, left, right, preferred_element_type=jnp.float32)  161 us
    unnamed x173, local copies, waits for them, and re-layouts  59.6 us
  transfers between devices with their start and end apart: 14, of which 7 were waited for; matrix products, arithmetic and copies ran while one was open for 21% of the time, Pallas kernels for 0%

commit v1 on v0

--- a/solution.py
+++ b/solution.py
@@ -53,12 +53,6 @@
     return jnp.concatenate(
         [first * cosine - second * sine, second * cosine + first * sine], axis=-1
     )
-
-
-def spread_out(local_grad, picked, lead):
-    if lead:
-        return picked[None, :, None, None] * local_grad[:, None]
-    return picked[:, None, None] * local_grad[None]
 
 
 def per_device(
@@ -95,7 +89,6 @@
     width_pick = lax.dynamic_index_in_dim(upper_width, chosen, 1, keepdims=False)
     keys_pick = lax.dynamic_index_in_dim(upper_keys, chosen, 1, keepdims=False)
     hidden_pick = lax.dynamic_index_in_dim(upper_hidden, chosen, 1, keepdims=False)
-    picked = (jnp.arange(NAD, dtype=jnp.int32) == chosen).astype(jnp.float32)
     positions = lax.dynamic_slice_in_dim(positions_of(segments), offset, tok_rows)
     cosine, sine = angles(positions, HD)
     padded_segs = jnp.concatenate([jnp.full((tok_rows,), -1, jnp.int32), segments])
@@ -298,36 +291,56 @@
     attn_width_local = jnp.stack([width_query_grad, width_out_grad])
     lower_local = jnp.concatenate([attn_lower_local, ffn_lower_local], axis=0)
     width_local = jnp.concatenate([attn_width_local, width_down_grad[None]], axis=0)
-    lower_dense = spread_out(lower_local, picked, True)
-    down_dense = spread_out(down_lower_grad, picked, False)
-    width_dense = spread_out(width_local, picked, True)
-    keys_dense = spread_out(keys_local, picked, True)
-    hidden_dense = spread_out(hidden_local, picked, True)
-    lower_part, down_part, width_part, keys_part, hidden_part = (
-        lax.psum_scatter(
-            lower_dense.astype(jnp.bfloat16), "grp", scatter_dimension=1, tiled=True
-        ).astype(jnp.float32),
-        lax.psum_scatter(
-            down_dense.astype(jnp.bfloat16), "grp", scatter_dimension=0, tiled=True
-        ).astype(jnp.float32),
-        lax.psum_scatter(
-            width_dense.astype(jnp.bfloat16), "grp", scatter_dimension=1, tiled=True
-        ).astype(jnp.float32),
-        lax.psum_scatter(
-            keys_dense.astype(jnp.bfloat16), "grp", scatter_dimension=1, tiled=True
-        ).astype(jnp.float32),
-        lax.psum_scatter(
-            hidden_dense.astype(jnp.bfloat16), "grp", scatter_dimension=1, tiled=True
-        ).astype(jnp.float32),
-    )
-    lower_sum, down_sum, width_sum, keys_sum, hidden_sum = (
-        lax.psum_scatter(lower_part, "rep", scatter_dimension=2, tiled=True),
-        lax.psum_scatter(down_part, "rep", scatter_dimension=1, tiled=True),
-        lax.psum_scatter(width_part, "rep", scatter_dimension=3, tiled=True),
-        lax.psum_scatter(keys_part, "rep", scatter_dimension=3, tiled=True),
-        lax.psum_scatter(hidden_part, "rep", scatter_dimension=3, tiled=True),
-    )
-    return (layer_out, input_grad, lower_sum, down_sum, width_sum, keys_sum, hidden_sum)
+    sums = summed_by_adapter(
+        [
+            lower_local.transpose(0, 2, 1),
+            down_lower_grad.T[None],
+            width_local,
+            keys_local,
+            hidden_local,
+        ],
+        chosen,
+    )
+    return (
+        layer_out,
+        input_grad,
+        sums[0].transpose(0, 1, 3, 2),
+        sums[1][0].transpose(0, 2, 1),
+        sums[2],
+        sums[3],
+        sums[4],
+    )
+
+
+def summed_by_adapter(parts, chosen):
+    reps = lax.axis_size("rep")
+    pieces = [part.shape[-1] // reps for part in parts]
+    blocks = [
+        part.reshape(-1, reps, piece).transpose(1, 0, 2).reshape(reps, -1)
+        for part, piece in zip(parts, pieces)
+    ]
+    mine = jnp.concatenate(blocks, axis=1)
+    other = lax.ppermute(mine.astype(jnp.bfloat16), "grp", [(0, 1), (1, 0)])
+    both = (mine + other.astype(jnp.float32)).astype(jnp.bfloat16)
+    label = jnp.full((reps, 128), chosen, jnp.int32).astype(jnp.bfloat16)
+    received = lax.all_to_all(
+        jnp.concatenate([label, both], axis=1), "rep", 0, 0, tiled=True
+    )
+    quota = NAD // lax.axis_size("grp")
+    wanted = lax.axis_index("grp") * quota + jnp.arange(quota, dtype=jnp.int32)
+    picks = (received[:, 0].astype(jnp.int32)[None, :] == wanted[:, None]).astype(jnp.bfloat16)
+    total = jnp.dot(picks, received[:, 128:], preferred_element_type=jnp.float32)
+    outs = []
+    start = 0
+    for part, piece in zip(parts, pieces):
+        count = part.shape[0] * part.shape[1] * piece
+        outs.append(
+            total[:, start : start + count]
+            .reshape(quota, part.shape[0], part.shape[1], piece)
+            .transpose(1, 0, 2, 3)
+        )
+        start += count
+    return outs
 
 
 def solution(mesh):

time: 880 us -> 423 us (0.48)
  waiting for transfers between devices: 482 us -> 18.5 us
  local copies, waits for them, and re-layouts: 81.2 us -> 66.7 us
  matrix products: 220 us -> 234 us
  starting transfers between devices: 6.54 us -> 16.7 us
    unnamed x15 -> x4, waiting for transfers between devices: 476 us -> 2.58 us
    unnamed x173 -> x140, local copies, waits for them, and re-layouts: 59.6 us -> 15.9 us
    reshape x0 -> x17, local copies, waits for them, and re-layouts: none -> 17.5 us  [the longest x9 14.3 us: summed_by_adapter(): part.reshape(-1, reps, piece).transpose(1, 0, 2).reshape(reps, -1)]
    all_to_all x0 -> x1, waiting for transfers between devices: none -> 13.6 us  [summed_by_adapter(): lax.all_to_all(jnp.concatenate([label, both], axis=1), 'rep', 0, 0, tiled...]
    convert_element_type x10 -> x3, other arithmetic: 12.3 us -> 0.35 us  [the longest x1 0.17 us: summed_by_adapter(): both = (mine + other.astype(jnp.float32)).astype(jnp.bfloat16)]
    dot_general x68, matrix products: 161 us -> 172 us  [contract(): return jnp.einsum(form, left, right, preferred_element_type=jnp.float32)]
  transfers between devices with their start and end apart: 14 -> 10, of which waited for: 7 -> 2; matrix products, arithmetic and copies ran while one was open for 21% -> 33% of each run, Pallas kernels for 0% -> 0%
where the time goes in v1:
time: 423 us; the launch traced here: 415 us
  matrix products  234 us (55%)
  local copies, waits for them, and re-layouts  66.7 us (16%)
  other arithmetic  61.4 us (15%)
  waiting for transfers between devices  18.5 us (4%)
  starting transfers between devices  16.7 us (4%)
  between operations  15.6 us (4%)
    dot_general x68, matrix products, contract(): return jnp.einsum(form, left, right, preferred_element_type=jnp.float32)  172 us
    unnamed x140, local copies, waits for them, and re-layouts  15.9 us
    dot_general x1, matrix products, per_device(): jnp.dot(normed_two, gate_up_full, preferred_element_type=jnp.float32)  14.8 us
    reshape x9, local copies, waits for them, and re-layouts, summed_by_adapter(): part.reshape(-1, reps, piece).transpose(1, 0, 2).reshape(reps, -1)  14.3 us
    all_to_all x1, waiting for transfers between devices, summed_by_adapter(): lax.all_to_all(jnp.concatenate([label, both], axis=1), 'rep', 0, 0, tiled...  13.6 us
    convert_element_type x6, other arithmetic, head_backward(): grad_scores = (chances * (grad_chances - jnp.sum(chances * grad_chances,...  11.9 us
    dot_general x1, matrix products, per_device(): jnp.dot(active, down_full, preferred_element_type=jnp.float32)  10.4 us
    and x12, other arithmetic, per_device(): (key_place[None, :] <= query_place[:, None]) & (key_segs[None, :] == quer...  9.94 us
  transfers between devices with their start and end apart: 10, of which 2 were waited for; matrix products, arithmetic and copies ran while one was open for 33% of the time, Pallas kernels for 0%

profile of v1, /device:TPU:0, one launch (start us, length us, event | category | flops | bytes accessed | tf_op | source)
XLA Modules:
  0.0 415.3 jit_solution(4619235780139165903)
XLA Ops:
  18.0 2.5 fusion.108
  26.3 5.2 %fusion.115 = f32[512,1920]{1,0:T(8,128)S(1)} fusion(bf16[1152,1920]{1,0:T(8,128)(2,1)} %all-gather.6.cloned.1.call-done, bf16[1,512,1152]{2,1,0:T(8,128)(2,1)} %param.18, f32[1152]{0:T(1024)S(1)} %get-tuple-element.163, f32[512]{0:T(512)S(1)} %fusion.155), kind=kOutput, calls=%fused_computation.176 | convolution fusion | flops 2267283456 | bytes 9542144 | tf_op jit(solution)/shard_map/dot_general | solution.py:108
  31.5 2.7 convolution_add_fusion.5
  37.0 3.4 copy.131
  53.4 48.2 %while.30 = (s32[]{:T(128)}, bf16[6,512,3,64]{1,3,2,0:T(8,128)(2,1)S(1)}, f32[6,3,512]{2,1,0:T(4,128)}, bf16[6,1024,64]{1,2,0:T(8,128)(2,1)}, bf16[6,1024,64]{1,...) while((s32[]{:T(128)}, ...), condition=%wide.region_6.7_spmd.clone.clone, body=%wide.region_3.6_spmd.clone.sunk.clone | while | flops 423098880 | bytes 21893732 | solution.py:149
  58.5 2.9 fusion.250
  66.5 2.9 fusion.250
  74.6 3.0 fusion.250
  82.6 2.9 fusion.250
  90.7 2.9 fusion.250
  98.7 2.9 fusion.250
  103.3 3.7 fusion.170
  107.1 2.8 multiply_reduce_fusion.1
  114.0 6.5 %fusion.104 = f32[512,3072]{1,0:T(8,128)S(1)} fusion(bf16[3072,1152]{1,0:T(8,128)(2,1)} %all-gather.12.cloned.1.call-done, bf16[1,512,1152]{2,1,0:T(8,128)(2,1)S(1)} %copy-done.9), kind=kOutput, calls=%fused_computation.136 | convolution fusion | flops 3623878656 | bytes 14548992 | tf_op jit(solution)/shard_map/td,fd->tf/dot_general | solution.py:28
  120.6 4.5 %convolution_add_fusion = f32[512,3072]{1,0:T(8,128)} fusion(f32[512,3072]{1,0:T(8,128)S(1)} %fusion.104, bf16[16,512]{1,0:T(8,128)(2,1)S(1)} %copy-done.45, bf16[8,3072,16]{1,2,0:T(8,128)(2,1)} %param.28, s32[]{:T(128)S(6)} %select_n.31), kind=kOutput, calls=%fused_computation.78 | convolution fusion | flops 51904512 | bytes 12697604 | tf_op jit(solution)/shard_map/tr,fr->tf/dot_general | solution.py:28
  125.1 14.8 %fusion.171 = f32[512,6144]{1,0:T(8,128)} fusion(bf16[512,1152]{1,0:T(8,128)(2,1)} %copy-done.10, bf16[1152,6144]{1,0:T(8,128)(2,1)} %all-gather.10.cloned.1.call-done), kind=kOutput, calls=%fused_computation.281 | convolution fusion | flops 7247757312 | bytes 27918336 | tf_op jit(solution)/shard_map/dot_general | solution.py:163
  139.9 3.9 slice_add_fusion
  144.5 7.0 %multiply_convert_fusion.1 = (bf16[512,3072]{1,0:T(8,128)(2,1)S(1)}, bf16[512,3072]{1,0:T(8,128)(2,1)}, bf16[512,3072]{1,0:T(8,128)(2,1)S(1)}) fusion(f32[512,3072]{1,0:T(8,128)S(1)} %copy-done.14, f32[512,3072]{1,0:T(8,128)S(1)} %slice_add_fusion, bf16[2,8,16,3072]{3,2,1,0:T(8,128)(2,1)S(1)} %copy-done, s32[]{:T(128)S(6)} %select_n.31, ...), kind=kOutput, calls=%fused_computation.75 | convolution fusion | flops 77070336 | bytes 28426244 | tf_op jit(solution)/shard_map/dot_general | solution.py:164
  157.3 16.9 %multiply_reduce_fusion = (f32[512]{0:T(512)}, f32[512,1152]{1,0:T(8,128)}) fusion(f32[512,1152]{1,0:T(8,128)} %get-tuple-element.234, f32[1152]{0:T(1024)} %get-tuple-element.162, f32[512,1152]{1,0:T(8,128)S(1)} %fusion.121, bf16[1152,6144]{1,0:T(8,128)(2,1)} %all-gather.10.cloned.1.call-done, bf16[512,3072]{1,0:T(8,128)(2,1)} %copy-done.4, ...), kind=kOutput, calls=%fused_computation.112 | convolution fusion | flops 7262699008 | bytes 27531776 | tf_op jit(solution)/shard_map/tf,df->td/dot_general | solution.py:28
  174.8 3.1 fusion.88
  185.8 100.1 %while.31 = (s32[]{:T(128)}, f32[6,512,3,64]{1,3,2,0:T(8,128)}, f32[6,1024,64]{1,2,0:T(8,128)}, f32[6,1024,64]{1,2,0:T(8,128)}, bf16[6,1024,64]{1,2,0:T(8,128)(2...) while((s32[]{:T(128)}, f32[6,512,3,64]{1,3,2,0:T(8,128)}, ...), condition=%wide.region_11.12_spmd.clone.clone, body=%wide.region_9.11_spmd.clone.sunk.clone | while | flops 1031961088 | bytes 51440768 | solution.py:246
  189.7 2.9 fusion.260
  197.0 2.7 fusion.263
  199.7 3.1 fusion.264
  206.3 2.9 fusion.260
  213.6 2.7 fusion.263
  216.3 3.1 fusion.264
  223.0 2.9 fusion.260
  230.2 2.7 fusion.263
  232.9 3.1 fusion.264
  239.5 2.9 fusion.260
  246.8 2.7 fusion.263
  249.5 3.1 fusion.264
  256.2 2.9 fusion.260
  263.4 2.7 fusion.263
  266.1 3.1 fusion.264
  272.8 2.9 fusion.260
  280.0 2.7 fusion.263
  282.7 3.1 fusion.264
  315.7 10.4 %convolution_add_fusion.6 = f32[512,1152]{1,0:T(8,128)} fusion(f32[512,1152]{1,0:T(8,128)} %get-tuple-element.234, bf16[512,3072]{1,0:T(8,128)(2,1)} %get-tuple-element.215, bf16[3072,1152]{1,0:T(8,128)(2,1)} %all-gather.12.cloned.1.call-done), kind=kOutput, calls=%fused_computation.92 | convolution fusion | flops 3624468480 | bytes 14942208 | tf_op jit(solution)/shard_map/dot_general | solution.py:176
  343.8 2.5 reshape.337
  356.0 2.7 collective-permute-start.4
  361.0 6.6 %fusion.91 = f32[512,1152]{1,0:T(8,128)} fusion(bf16[1152,1920]{1,0:T(8,128)(2,1)} %all-gather.6.cloned.1.call-done, bf16[512,384]{0,1:T(8,128)(2,1)S(1)} %copy-done.19, bf16[512,384]{0,1:T(8,128)(2,1)S(1)} %bitcast.442, bf16[512,1152]{0,1:T(8,128)(2,1)S(1)} %bitcast.437), kind=kOutput, calls=%fused_computation.120 | convolution fusion | flops 2270822400 | bytes 8749056 | tf_op jit(solution)/shard_map/te,de->td/dot_general | solution.py:28
  369.1 2.9 reduce.10
  374.3 7.2 %all-to-all-start = ((bf16[16,2,10240]{2,1,0:T(2,128)(2,1)}), bf16[16,2,10240]{2,1,0:T(2,128)(2,1)}, u32[]{:S(2)}, u32[]{:S(2)}) async-start(bf16[16,2,10240]{2,1,0:T(2,128)(2,1)} %reshape.368), calls=%async_computation | async-start | bytes 1310720 | tf_op jit(solution)/shard_map/all_to_all | solution.py:326
  381.6 2.5 fusion.85
  385.7 13.6 %all-to-all-done = bf16[16,2,10240]{2,1,0:T(2,128)(2,1)} async-done(((bf16[16,2,10240]{2,1,0:T(2,128)(2,1)}), bf16[16,2,10240]{2,1,0:T(2,128)(2,1)}, u32[]{:S(2)}, u32[]{:S(2)}) %all-to-all-start) | async-done | bytes 655392 | tf_op jit(solution)/shard_map/all_to_all | solution.py:326
  399.2 4.2 %reshape.369 = bf16[16,1,20480]{2,1,0:T(2,128)(2,1)S(1)} reshape(bf16[16,2,10240]{2,1,0:T(2,128)(2,1)} %all-to-all-done) | data formatting | bytes 1310720
  (330 shorter events, 199.4 us)
Async XLA Ops:
  7.2 132.7 %copy-start = (bf16[2,8,16,3072]{3,2,1,0:T(8,128)(2,1)S(1)}, bf16[2,8,16,3072]{3,2,1,0:T(8,128)(2,1)}, u32[]{:S(2)}) copy-start(bf16[2,8,16,3072]{3,2,1,0:T(8,128)(2,1)} %param.31) | copy-start | bytes 4718596
  7.2 19.1 %all-gather.6.cloned.1.call-start = ((), (), s32[]{:S(2)}) async-start(), calls=%async_computation.1 | async-start | bytes 6635520 | tf_op jit(solution)/shard_map/all_gather | solution.py:82
  7.9 95.4 %all-gather.8.cloned.1.call-start = ((), (), s32[]{:S(2)}) async-start(), calls=%async_computation.2 | async-start | bytes 3981312 | tf_op jit(solution)/shard_map/all_gather | solution.py:83
  8.7 105.4 %all-gather.12.cloned.1.call-start = ((), (), s32[]{:S(2)}) async-start(), calls=%async_computation.4 | async-start | bytes 10616832 | tf_op jit(solution)/shard_map/all_gather | solution.py:85
  9.4 115.7 %all-gather.10.cloned.1.call-start = ((), (), s32[]{:S(2)}) async-start(), calls=%async_computation.3 | async-start | bytes 21233664 | tf_op jit(solution)/shard_map/all_gather | solution.py:84
  10.0 5.1 %copy-start.55 = (s32[1,1024]{1,0:T(1,128)S(1)}, s32[1,1024]{1,0:T(1,128)}, u32[]{:S(2)}) copy-start(s32[1,1024]{1,0:T(1,128)} %param.20) | copy-start | bytes 12292
  13.5 12.8 %copy-start.56 = (f32[1152]{0:T(1024)}, f32[1152]{0:T(1024)S(1)}, u32[]{:S(2)}) copy-start(f32[1152]{0:T(1024)S(1)} %get-tuple-element.163) | copy-start | bytes 13828
  15.1 16.4 %copy-start.62 = (f32[512]{0:T(512)}, f32[512]{0:T(512)S(1)}, u32[]{:S(2)}) copy-start(f32[512]{0:T(512)S(1)} %fusion.155) | copy-start | bytes 6148
  22.1 9.5 %copy-start.52 = (bf16[1152,16]{0,1:T(8,128)(2,1)}, bf16[1152,16]{0,1:T(8,128)(2,1)S(1)}, u32[]{:S(2)}) copy-start(bf16[1152,16]{0,1:T(8,128)(2,1)S(1)} %get-tuple-element.222) | copy-start | bytes 110596
  22.1 9.5 %copy-start.53 = (bf16[1152,16]{0,1:T(8,128)(2,1)}, bf16[1152,16]{0,1:T(8,128)(2,1)S(1)}, u32[]{:S(2)}) copy-start(bf16[1152,16]{0,1:T(8,128)(2,1)S(1)} %get-tuple-element.223) | copy-start | bytes 110596
  22.1 9.5 %copy-start.54 = (bf16[1152,16]{0,1:T(8,128)(2,1)}, bf16[1152,16]{0,1:T(8,128)(2,1)S(1)}, u32[]{:S(2)}) copy-start(bf16[1152,16]{0,1:T(8,128)(2,1)S(1)} %get-tuple-element.224) | copy-start | bytes 110596
  24.0 7.5 %copy-start.43 = (bf16[512,48]{0,1:T(8,128)(2,1)}, bf16[512,48]{0,1:T(8,128)(2,1)S(1)}, u32[]{:S(2)}) copy-start(bf16[512,48]{0,1:T(8,128)(2,1)S(1)} %convolution_convert_fusion) | copy-start | bytes 147460
  42.8 7.0 %collective-permute-start.1 = (bf16[512,384]{0,1:T(8,128)(2,1)S(1)}, bf16[512,384]{0,1:T(8,128)(2,1)S(1)}, u32[]{:S(2)}, u32[]{:S(2)}) collective-permute-start(bf16[512,384]{0,1:T(8,128)(2,1)S(1)} %bitcast.454), channel_id=1, source_target_pairs={{0,16},{1,17},{2,18},{3,19},{4,20},{5,21},{6,22},{7,23},{8,24},{9,... | collective-permute-start | bytes 1179656 | tf_op jit(solution)/shard_map/ppermute | solution.py:24
  44.9 5.1 %collective-permute-start = (bf16[512,384]{1,0:T(8,128)(2,1)}, bf16[512,384]{1,0:T(8,128)(2,1)S(1)}, u32[]{:S(2)}, u32[]{:S(2)}) collective-permute-start(bf16[512,384]{1,0:T(8,128)(2,1)} %fusion.97), channel_id=1, source_target_pairs={{0,16},{1,17},{2,18},{3,19},{4,20},{5,21},{6,22},{7,23},{8,24},{9,... | collective-permute-start | bytes 1179656 | tf_op jit(solution)/shard_map/ppermute | solution.py:24
  101.6 5.4 %copy-start.5 = (bf16[6,512,3,64]{1,3,2,0:T(8,128)(2,1)}, bf16[6,512,3,64]{1,3,2,0:T(8,128)(2,1)S(1)}, u32[]{:S(2)}) copy-start(bf16[6,512,3,64]{1,3,2,0:T(8,128)(2,1)S(1)} %get-tuple-element.99) | copy-start | bytes 3538948
  101.6 5.4 %copy-start.15 = (bf16[6,1024,64]{1,2,0:T(8,128)(2,1)}, bf16[6,1024,64]{1,2,0:T(8,128)(2,1)S(1)}, u32[]{:S(2)}) copy-start(bf16[6,1024,64]{1,2,0:T(8,128)(2,1)S(1)} %get-tuple-element.519) | copy-start | bytes 2359300
  103.3 3.8 copy-start.7
  103.3 3.8 copy-start.47
  109.9 3.7 copy-start.34
  109.9 3.7 copy-start.36
  114.0 6.6 %copy-start.45 = (bf16[16,512]{1,0:T(8,128)(2,1)S(1)}, bf16[16,512]{1,0:T(8,128)(2,1)}, u32[]{:S(2)}) copy-start(bf16[16,512]{1,0:T(8,128)(2,1)} %fusion.108) | copy-start | bytes 49156
  139.9 4.6 %copy-start.14 = (f32[512,3072]{1,0:T(8,128)S(1)}, f32[512,3072]{1,0:T(8,128)}, u32[]{:S(2)}) copy-start(f32[512,3072]{1,0:T(8,128)} %convolution_add_fusion) | copy-start | bytes 18874372
  151.5 4.7 %copy-start.3 = (bf16[512,3072]{1,0:T(8,128)(2,1)}, bf16[512,3072]{1,0:T(8,128)(2,1)S(1)}, u32[]{:S(2)}) copy-start(bf16[512,3072]{1,0:T(8,128)(2,1)S(1)} %get-tuple-element.214) | copy-start | bytes 9437188
  151.5 4.7 %copy-start.4 = (bf16[512,3072]{1,0:T(8,128)(2,1)}, bf16[512,3072]{1,0:T(8,128)(2,1)S(1)}, u32[]{:S(2)}) copy-start(bf16[512,3072]{1,0:T(8,128)(2,1)S(1)} %get-tuple-element.216) | copy-start | bytes 9437188
  174.8 4.2 %copy-start.22 = (bf16[1152,1152]{1,0:T(8,128)(2,1)S(1)}, bf16[1152,1152]{1,0:T(8,128)(2,1)}, u32[]{:S(2)}) copy-start(bf16[1152,1152]{1,0:T(8,128)(2,1)} %all-gather.8.cloned.1.call-done) | copy-start | bytes 7962628
  285.9 8.2 %copy-start.48 = (bf16[512,16]{0,1:T(8,128)(2,1)S(1)}, bf16[512,16]{0,1:T(8,128)(2,1)}, u32[]{:S(2)}) copy-start(bf16[512,16]{0,1:T(8,128)(2,1)} %convolution_convert_fusion.3) | copy-start | bytes 49156
  289.9 5.1 %copy-start.23 = (f32[6,512,3,64]{1,3,2,0:T(8,128)S(1)}, f32[6,512,3,64]{1,3,2,0:T(8,128)}, u32[]{:S(2)}) copy-start(f32[6,512,3,64]{1,3,2,0:T(8,128)} %get-tuple-element.101) | copy-start | bytes 7077892
  289.9 5.1 %copy-start.25 = (f32[512,32]{0,1:T(8,128)S(1)}, f32[512,32]{0,1:T(8,128)}, u32[]{:S(2)}) copy-start(f32[512,32]{0,1:T(8,128)} %get-tuple-element.232) | copy-start | bytes 196612
  289.9 5.1 %copy-start.31 = (f32[512,32]{0,1:T(8,128)S(1)}, f32[512,32]{0,1:T(8,128)}, u32[]{:S(2)}) copy-start(f32[512,32]{0,1:T(8,128)} %get-tuple-element.230) | copy-start | bytes 196612
  295.4 3.8 copy-start.2
  295.5 5.5 %copy-start.12 = (bf16[512,18,64]{0,2,1:T(8,128)(2,1)}, bf16[512,18,64]{0,2,1:T(8,128)(2,1)S(1)}, u32[]{:S(2)}) copy-start(bf16[512,18,64]{0,2,1:T(8,128)(2,1)S(1)} %maximum_convert_fusion) | copy-start | bytes 3538948
  309.3 19.0 %collective-permute-start.2 = (bf16[512,384]{0,1:T(8,128)(2,1)}, bf16[512,384]{0,1:T(8,128)(2,1)}, u32[]{:S(2)}, u32[]{:S(2)}) collective-permute-start(bf16[512,384]{0,1:T(8,128)(2,1)} %bitcast.461), channel_id=1, source_target_pairs={{16,0},{17,1},{18,2},{19,3},{20,4},{21,5},{22,6},{23,7},{24,8},{25... | collective-permute-start | bytes 1179656 | tf_op jit(solution)/shard_map/ppermute | solution.py:24
  310.6 21.3 %collective-permute-start.3 = (bf16[512,384]{0,1:T(8,128)(2,1)}, bf16[512,384]{0,1:T(8,128)(2,1)}, u32[]{:S(2)}, u32[]{:S(2)}) collective-permute-start(bf16[512,384]{0,1:T(8,128)(2,1)} %bitcast.460), channel_id=1, source_target_pairs={{16,0},{17,1},{18,2},{19,3},{20,4},{21,5},{22,6},{23,7},{24,8},{25... | collective-permute-start | bytes 1179656 | tf_op jit(solution)/shard_map/ppermute | solution.py:24
  315.7 10.4 %copy-start.6 = (bf16[6,512,3,64]{1,3,2,0:T(8,128)(2,1)S(1)}, bf16[6,512,3,64]{1,3,2,0:T(8,128)(2,1)}, u32[]{:S(2)}) copy-start(bf16[6,512,3,64]{1,3,2,0:T(8,128)(2,1)} %copy-done.5) | copy-start | bytes 3538948
  315.7 10.4 %copy-start.50 = (bf16[512,16]{0,1:T(8,128)(2,1)S(1)}, bf16[512,16]{0,1:T(8,128)(2,1)}, u32[]{:S(2)}) copy-start(bf16[512,16]{0,1:T(8,128)(2,1)} %copy-done.49) | copy-start | bytes 49156
  315.7 11.5 %copy-start.11 = (bf16[512,1152]{1,0:T(8,128)(2,1)S(1)}, bf16[512,1152]{1,0:T(8,128)(2,1)}, u32[]{:S(2)}) copy-start(bf16[512,1152]{1,0:T(8,128)(2,1)} %copy-done.10) | copy-start | bytes 3538948
  315.7 11.5 %copy-start.40 = (bf16[512,16]{0,1:T(8,128)(2,1)S(1)}, bf16[512,16]{0,1:T(8,128)(2,1)}, u32[]{:S(2)}) copy-start(bf16[512,16]{0,1:T(8,128)(2,1)} %copy-done.39) | copy-start | bytes 49156
  315.7 11.5 %copy-start.42 = (bf16[512,16]{0,1:T(8,128)(2,1)S(1)}, bf16[512,16]{0,1:T(8,128)(2,1)}, u32[]{:S(2)}) copy-start(bf16[512,16]{0,1:T(8,128)(2,1)} %copy-done.41) | copy-start | bytes 49156
  329.6 12.1 %copy-start.8 = (bf16[1,512,1152]{2,1,0:T(8,128)(2,1)S(1)}, bf16[1,512,1152]{2,1,0:T(8,128)(2,1)}, u32[]{:S(2)}) copy-start(bf16[1,512,1152]{2,1,0:T(8,128)(2,1)} %param.18) | copy-start | bytes 3538948
  350.9 7.7 %copy-start.24 = (f32[512,1152]{1,0:T(8,128)S(1)}, f32[512,1152]{1,0:T(8,128)}, u32[]{:S(2)}) copy-start(f32[512,1152]{1,0:T(8,128)} %convolution_add_fusion.6) | copy-start | bytes 7077892
  355.9 5.1 %copy-start.13 = (bf16[512,18,64]{0,2,1:T(8,128)(2,1)S(1)}, bf16[512,18,64]{0,2,1:T(8,128)(2,1)}, u32[]{:S(2)}) copy-start(bf16[512,18,64]{0,2,1:T(8,128)(2,1)} %copy-done.12) | copy-start | bytes 3538948
  355.9 5.1 %copy-start.17 = (bf16[512,6,64]{0,2,1:T(8,128)(2,1)S(1)}, bf16[512,6,64]{0,2,1:T(8,128)(2,1)}, u32[]{:S(2)}) copy-start(bf16[512,6,64]{0,2,1:T(8,128)(2,1)} %copy-done.16) | copy-start | bytes 1179652
  355.9 5.1 %copy-start.19 = (bf16[512,384]{0,1:T(8,128)(2,1)S(1)}, bf16[512,384]{0,1:T(8,128)(2,1)}, u32[]{:S(2)}) copy-start(bf16[512,384]{0,1:T(8,128)(2,1)} %copy-done.18) | copy-start | bytes 1179652
  356.0 11.5 %collective-permute-start.4 = (bf16[16,20352]{1,0:T(8,128)(2,1)S(1)}, bf16[16,20352]{1,0:T(8,128)(2,1)S(1)}, u32[]{:S(2)}, u32[]{:S(2)}) collective-permute-start(bf16[16,20352]{1,0:T(8,128)(2,1)S(1)} %convert_element_type.211), channel_id=1, source_target_pairs={{0,16},{16,0},{1,17},{17,1},{2,18},{18,2},{3,19},{19,3},{4,20},{20... | collective-permute-start | bytes 1953800 | tf_op jit(solution)/shard_map/ppermute | solution.py:323
  367.7 13.9 %copy-start.51 = (bf16[512,16]{0,1:T(8,128)(2,1)S(1)}, bf16[512,16]{0,1:T(8,128)(2,1)}, u32[]{:S(2)}) copy-start(bf16[512,16]{0,1:T(8,128)(2,1)} %convolution_convert_fusion.2) | copy-start | bytes 49156
  374.3 24.9 %all-to-all-start = ((bf16[16,2,10240]{2,1,0:T(2,128)(2,1)}), bf16[16,2,10240]{2,1,0:T(2,128)(2,1)}, u32[]{:S(2)}, u32[]{:S(2)}) async-start(bf16[16,2,10240]{2,1,0:T(2,128)(2,1)} %reshape.368), calls=%async_computation | async-start | bytes 1310720 | tf_op jit(solution)/shard_map/all_to_all | solution.py:326
  385.7 18.6 %copy-start.65 = (s32[4]{0:T(128)S(1)}, s32[4]{0:T(128)}, u32[]{:S(2)}) copy-start(s32[4]{0:T(128)} %iota_add_fusion.2) | copy-start | bytes 52
  399.2 9.3 %copy-start.1 = (bf16[2,8,16,3072]{3,2,1,0:T(8,128)(2,1)S(1)}, bf16[2,8,16,3072]{3,2,1,0:T(8,128)(2,1)}, u32[]{:S(2)}) copy-start(bf16[2,8,16,3072]{3,2,1,0:T(8,128)(2,1)} %param.31) | copy-start | bytes 4718596
  (28 other events, 53.1 us)
Sparse Core Ops, SparseCore 0:
  9.6 16.7 all-gather.5
  27.9 12.5 all-gather.7
  42.0 19.0 all-gather.11
  62.5 27.6 all-gather.9
